TPU v7x, 32 devices: a whole 2x2x4 slice. The times are simulated.
32 devices in a mesh: dp: 16 (over z, y, x), blk: 2 (over core).
Axes of the slice: x: 2, y: 2, z: 4, core: 2. Of those that a mesh axis runs over, the one named last changes fastest.
Arguments:
- vectors: float32 [16384, 96], P('dp'), may hold values from -16 to 16
- codes: int32 [16384, 8], P('dp'), may hold values from 0 to 255, as said below
- weights: bfloat16 [16384], P('dp'), may hold values from 0.25 to 4
- ridge: float32 [1], replicated, may hold values from 0.1 to 0.5
Outputs:
- codebooks: float32 [8, 256, 96], replicated
- residual: float32 [16384, 96], P('dp')
- distortion: float32 [], replicated
Inputs may be any that keep to these rules, and one draw needn't show every extreme that they name: `codes`: 8 codebook indices per vector.
All inputs are finite; a program needn't handle non-finite values.
Results may differ from a plain program's by a relative error of at most 0.0003.
Values sent between devices are 32-bit elements; how exact they have to be, the bound alone decides.
A program may use at most 128 MiB of HBM per device.

v0:
```python
import jax
import jax.numpy as jnp
from jax import lax
from jax.sharding import PartitionSpec as P

K = 256
M = 8
ITERS = 8


HIGH = lax.Precision.HIGHEST


def partner_2(array, axis, bit):
    return lax.ppermute(array, axis, [(i, i ^ 1 << bit) for i in range(lax.axis_size(axis))])


def pair_books(half):
    local = jnp.array([0, 0, 0, 1, 1, 1, 2, 2, 2, 3, 3, 3], jnp.int32)
    spread = jnp.array([1, 2, 3, 1, 2, 3, 1, 2, 3, 1, 2, 3], jnp.int32)
    near_first = local + 4 * half
    near_second = (near_first + spread) % 8
    far_first = jnp.array([0, 1], jnp.int32) + 2 * half
    firsts = jnp.concatenate([near_first, far_first])
    seconds = jnp.concatenate([near_second, far_first + 4])
    return (firsts, seconds)


def body(vectors, codes, weights, ridge):
    rows = vectors.shape[0]
    width = vectors.shape[1]
    half = lax.axis_index("blk")
    firsts, seconds = pair_books(half)
    npairs = firsts.shape[0]
    levels = lax.iota(jnp.int32, K)
    step_rows = min(512, rows)

    def accumulate(turn, carry):
        joint, right_part, count_part = carry
        start = turn * step_rows
        block_codes = lax.dynamic_slice_in_dim(codes, start, step_rows, 0)
        block_vectors = lax.dynamic_slice_in_dim(vectors, start, step_rows, 0)
        block_mass = lax.dynamic_slice_in_dim(weights, start, step_rows, 0)
        hot = (block_codes.T[:, :, None] == levels[None, None, :]).astype(jnp.bfloat16)
        first_hot = jnp.take(hot, firsts, axis=0) * block_mass[None, :, None]
        second_hot = jnp.take(hot, seconds, axis=0)
        joint = joint + jnp.einsum(
            "krc,kre->kce", first_hot, second_hot, preferred_element_type=jnp.float32
        )
        owned = lax.dynamic_slice_in_dim(hot, 4 * half, 4, 0).astype(jnp.float32)
        owned = owned * block_mass.astype(jnp.float32)[None, :, None]
        right_part = right_part + jnp.einsum("mrk,rd->mkd", owned, block_vectors, precision=HIGH)
        count_part = count_part + jnp.sum(owned, axis=1)
        return (joint, right_part, count_part)

    start_carry = (
        jnp.zeros((npairs, K, K), jnp.float32),
        jnp.zeros((4, K, width), jnp.float32),
        jnp.zeros((4, K), jnp.float32),
    )
    joint, right_part, count_part = lax.fori_loop(0, rows // step_rows, accumulate, start_carry)
    books = lax.iota(jnp.int32, M)
    pick_first = (firsts[:, None] == books[None, :]).astype(jnp.float32)
    pick_second = (seconds[:, None] == books[None, :]).astype(jnp.float32)
    joint, right_part, count_part = lax.psum((joint, right_part, count_part), "dp")
    right_all, count_all = (
        lax.all_gather(right_part, "blk", axis=0, tiled=True),
        lax.all_gather(count_part, "blk", axis=0, tiled=True),
    )
    total_mass = jnp.sum(count_all[0])
    lam = ridge[0] * total_mass / K
    precond = (count_all + lam)[:, :, None]
    solution = jnp.zeros((M, K, width), jnp.float32)
    remain = right_all
    scaled = remain / precond
    direction = scaled
    inner = jnp.sum(remain * scaled, axis=(0, 1))
    for step in range(ITERS):
        at_second = jnp.einsum("km,mcd->kcd", pick_second, direction, precision=HIGH)
        at_first = jnp.einsum("km,mcd->kcd", pick_first, direction, precision=HIGH)
        forward = jnp.einsum("kce,ked->kcd", joint, at_second, precision=HIGH)
        backward = jnp.einsum("kce,kcd->ked", joint, at_first, precision=HIGH)
        part = jnp.einsum("km,kcd->mcd", pick_first, forward, precision=HIGH)
        part = part + jnp.einsum("km,ked->med", pick_second, backward, precision=HIGH)
        partner = partner_2(part, "blk", 0)
        image = part + partner + precond * direction
        alpha = inner / jnp.sum(direction * image, axis=(0, 1))
        solution = solution + alpha * direction
        remain = remain - alpha * image
        scaled = remain / precond
        fresh = jnp.sum(remain * scaled, axis=(0, 1))
        direction = scaled + fresh / inner * direction
        inner = fresh
    recon = jnp.zeros_like(vectors)
    for book in range(M):
        recon = recon + jnp.take(solution[book], codes[:, book], axis=0)
    residual = vectors - recon
    mass = weights.astype(jnp.float32)
    total = lax.psum(jnp.sum(mass[:, None] * residual * residual), "dp")
    distortion = total / (total_mass * width)
    return (solution, residual, distortion)


def solution(mesh):
    return jax.shard_map(
        body,
        mesh=mesh,
        in_specs=(P("dp", None), P("dp", None), P("dp"), P()),
        out_specs=(P(), P("dp", None), P()),
        check_vma=False,
    )
```

profile of v0, /device:TPU:0, one launch (start us, length us, event | category | flops | bytes accessed | tf_op | source)
XLA Modules:
  0.0 443.0 jit_solution(15194481566728508207)
XLA Ops:
  8.1 34.0 %while.20 = (s32[]{:T(128)}, f32[14,256,256]{2,1,0:T(8,128)}, f32[4,256,96]{1,2,0:T(8,128)S(1)}, f32[4,256]{1,0:T(4,128)S(1)}, s32[1024,8]{0,1:T(8,128)}, /*inde...) while((s32[]{:T(128)}, f32[14,256,256]{2,1,0:T(8,128)}, ...), condition=%wide.region_2.4_spmd.clone, body=%wide.region_0.3_spmd.clone.sunk | while | flops 1555762944 | bytes 36194140 | solution.py:61
  10.7 1.7 fusion.245
  12.4 2.7 gather_fusion.1
  15.1 2.6 gather_fusion
  17.7 6.8 %select_add_fusion.11 = f32[14,256,256]{2,1,0:T(8,128)} fusion(f32[14,256,256]{2,1,0:T(8,128)} %get-tuple-element.470, pred[]{:T(512)S(6)} %compare.4, bf16[14,512,256]{2,1,0:T(8,128)(2,1)} %gather_fusion, pred[14]{0:T(512)(128)(4,1)S(1)} %get-tuple-element.450, bf16[14,512,256]{2,1,0:T(8,128)(2,1)} %gather_fusion.1, ...), kind=kOutput, calls=%fused_computation.16.clone.1 | convolution fusion | flops 946864128 | bytes 14681117 | tf_op jit(solution)/shard_map/while/body/eval_jaxpr/krc,kre->kce/dot_general | solution.py:47
  27.2 1.7 fusion.245
  28.9 2.7 gather_fusion.1
  31.6 2.6 gather_fusion
  34.2 7.9 %select_add_fusion.11 = f32[14,256,256]{2,1,0:T(8,128)} fusion(f32[14,256,256]{2,1,0:T(8,128)} %get-tuple-element.470, pred[]{:T(512)S(6)} %compare.4, bf16[14,512,256]{2,1,0:T(8,128)(2,1)} %gather_fusion, pred[14]{0:T(512)(128)(4,1)S(1)} %get-tuple-element.450, bf16[14,512,256]{2,1,0:T(8,128)(2,1)} %gather_fusion.1, ...), kind=kOutput, calls=%fused_computation.16.clone.1 | convolution fusion | flops 946864128 | bytes 14681117 | tf_op jit(solution)/shard_map/while/body/eval_jaxpr/krc,kre->kce/dot_general | solution.py:47
  43.5 45.8 %psum.29 = f32[4,256]{1,0:T(4,128)S(1)} all-reduce(f32[4,256]{1,0:T(4,128)S(1)} %get-tuple-element.265), channel_id=1, replica_groups=mesh['dp'=16,'blk'=2] {'dp'}, use_global_device_ids=true, to_apply=%region_4.6 | all-reduce | flops 1024 | bytes 8192 | tf_op jit(solution)/shard_map/psum | solution.py:65
  89.2 1.8 all-gather
  92.3 119.8 %all-reduce.3.cloned.1.call-done = (f32[4,256,96]{1,2,0:T(8,128)}, f32[14,256,256]{2,1,0:T(8,128)}) async-done(((f32[4,256,96]{1,2,0:T(8,128)}, f32[14,256,256]{2,1,0:T(8,128)}), (f32[4,256,96]{1,2,0:T(8,128)}, f32[14,256,256]{2,1,0:T(8,128)})) %all-reduce.3.cloned.1.call-update) | async-done | bytes 4063248 | tf_op jit(solution)/shard_map/psum | solution.py:65
  212.2 2.7 all_gather.6
  217.2 4.4 fusion.82
  221.6 3.1 fusion.80
  226.2 1.7 fusion.84
  228.0 2.1 collective-permute-done
  231.1 1.4 multiply_reduce_fusion.13
  234.7 3.1 fusion.76
  239.2 4.8 %fusion.78 = f32[14,256,96]{1,2,0:T(8,128)S(1)} fusion(f32[14,256,256]{2,1,0:T(8,128)S(1)} %copy-done, f32[14,256,96]{1,0,2:T(8,128)S(1)} %fusion.155), kind=kOutput, calls=%fused_computation.97 | convolution fusion | flops 1056964608 | bytes 6422528 | tf_op jit(solution)/shard_map/kce,ked->kcd/dot_general | solution.py:81
  244.0 1.4 fusion.87
  245.7 2.1 collective-permute-done.1
  248.6 1.4 multiply_reduce_fusion.11
  251.9 3.1 fusion.72
  256.5 4.5 %fusion.74 = f32[14,256,96]{1,2,0:T(8,128)S(1)} fusion(f32[14,256,256]{2,1,0:T(8,128)S(1)} %copy-done, f32[14,256,96]{1,0,2:T(8,128)S(1)} %fusion.152), kind=kOutput, calls=%fused_computation.93 | convolution fusion | flops 1056964608 | bytes 6422528 | tf_op jit(solution)/shard_map/kce,ked->kcd/dot_general | solution.py:81
  261.1 1.4 fusion.90
  262.7 2.1 collective-permute-done.2
  265.7 1.4 multiply_reduce_fusion.9
  269.0 3.1 fusion.68
  273.5 4.6 %fusion.70 = f32[14,256,96]{1,2,0:T(8,128)S(1)} fusion(f32[14,256,256]{2,1,0:T(8,128)S(1)} %copy-done, f32[14,256,96]{1,0,2:T(8,128)S(1)} %fusion.149), kind=kOutput, calls=%fused_computation.89 | convolution fusion | flops 1056964608 | bytes 6422528 | tf_op jit(solution)/shard_map/kce,ked->kcd/dot_general | solution.py:81
  278.1 1.4 fusion.93
  279.8 2.1 collective-permute-done.3
  282.7 1.4 multiply_reduce_fusion.7
  286.5 3.1 fusion.64
  291.1 4.8 %fusion.66 = f32[14,256,96]{1,2,0:T(8,128)S(1)} fusion(f32[14,256,256]{2,1,0:T(8,128)S(1)} %copy-done, f32[14,256,96]{1,0,2:T(8,128)S(1)} %fusion.146), kind=kOutput, calls=%fused_computation.85 | convolution fusion | flops 1056964608 | bytes 6422528 | tf_op jit(solution)/shard_map/kce,ked->kcd/dot_general | solution.py:81
  295.9 2.3 fusion.96
  301.8 2.2 multiply_reduce_fusion.6
  304.0 2.8 multiply_reduce_fusion.5
  309.0 3.1 fusion.60
  313.6 4.6 %fusion.62 = f32[14,256,96]{1,2,0:T(8,128)S(1)} fusion(f32[14,256,256]{2,1,0:T(8,128)S(1)} %copy-done.1, f32[14,256,96]{1,0,2:T(8,128)S(1)} %fusion.143), kind=kOutput, calls=%fused_computation.81 | convolution fusion | flops 1056964608 | bytes 6422528 | tf_op jit(solution)/shard_map/kce,ked->kcd/dot_general | solution.py:81
  318.1 1.4 fusion.99
  320.1 1.9 collective-permute-done.5
  322.7 1.4 multiply_reduce_fusion.3
  326.0 3.1 fusion.56
  329.2 1.6 fusion.24
  330.8 4.4 fusion.58
  335.2 1.4 fusion.102
  337.1 1.9 collective-permute-done.6
  339.8 1.4 multiply_reduce_fusion.1
  343.1 3.1 fusion.52
  346.3 1.7 fusion.20
  347.9 4.4 fusion.54
  354.3 1.9 collective-permute-done.7
  357.0 1.8 multiply_add_fusion
  361.3 2.8 gather_fusion.3
  364.1 2.8 gather_fusion.4
  366.9 2.8 gather_fusion.5
  369.7 2.8 gather_fusion.6
  372.6 4.0 gather_fusion.7
  376.5 4.0 gather_fusion.8
  380.5 4.0 gather_fusion.9
  384.5 4.0 gather_fusion.2
  388.5 4.1 fusion.108
  392.6 40.4 %psum.31 = f32[]{:T(128)} all-reduce(f32[]{:T(128)} %get-tuple-element.334), channel_id=1, replica_groups=mesh['dp'=16,'blk'=2] {'dp'}, use_global_device_ids=true, to_apply=%region_24.27 | all-reduce | flops 1 | bytes 8 | tf_op jit(solution)/shard_map/psum | solution.py:99
  (163 shorter events, 48.1 us)
Async XLA Ops:
  7.2 205.0 %all-reduce.3.cloned.1.call-start = ((), (), s32[]{:S(2)}) async-start(), calls=%async_computation | async-start | bytes 8126464 | tf_op jit(solution)/shard_map/psum | solution.py:65
  9.6 1.1 copy-start.7
  26.1 1.1 copy-start.7
  42.1 0.7 copy-start.4
  214.9 17.6 %copy-start.2 = (f32[8,256,96]{1,2,0:T(8,128)}, f32[8,256,96]{1,2,0:T(8,128)S(1)}, u32[]{:S(2)}) copy-start(f32[8,256,96]{1,2,0:T(8,128)S(1)} %all_gather.6) | copy-start | bytes 2359300
  214.9 2.3 copy-start
  227.8 2.4 collective-permute-start
  231.1 1.5 copy-start.12
  245.5 2.4 collective-permute-start.1
  248.6 1.4 copy-start.14
  262.5 2.4 collective-permute-start.2
  265.7 1.4 copy-start.16
  279.6 2.4 collective-permute-start.3
  282.7 1.4 copy-start.18
  284.2 0.5 copy-start.20
  284.2 1.5 copy-start.5
  295.9 2.5 copy-start.10
  295.9 3.1 copy-start.8
  298.3 3.5 collective-permute-start.4
  300.0 3.9 copy-start.21
  300.7 3.3 copy-start.6
  307.0 2.0 copy-start.1
  319.6 2.4 collective-permute-start.5
  336.6 2.4 collective-permute-start.6
  353.8 3.2 copy-start.3
  353.8 3.2 copy-start.13
  353.8 3.2 copy-start.15
  353.8 3.2 copy-start.17
  353.8 3.2 copy-start.19
  353.8 2.4 collective-permute-start.7
  384.5 4.0 copy-start.9
  384.5 4.0 copy-start.11
Sparse Core Ops, SparseCore 0:
  43.0 169.1 all-reduce.2
where the time goes:
time: 448 us; the launch traced here: 443 us
  waiting for transfers between devices  134 us (30%)
  matrix products  118 us (26%)
  blocking collectives  90.7 us (20%)
  local copies, waits for them, and re-layouts  46.5 us (10%)
  other arithmetic  32.8 us (7%)
  between operations  19 us (4%)
    psum x1, waiting for transfers between devices, body(): lax.psum((joint, right_part, count_part), 'dp')  120 us
    psum x1, blocking collectives, body(): lax.psum((joint, right_part, count_part), 'dp')  45.8 us
    psum x1, blocking collectives, body(): total = lax.psum(jnp.sum(mass[:, None] * residual * residual), 'dp')  40.4 us
    dot_general x8, matrix products, body(): forward = jnp.einsum('kce,ked->kcd', joint, at_second, precision=HIGH)  36.4 us
    gather x8, local copies, waits for them, and re-layouts, body(): recon = recon + jnp.take(solution[book], codes[:, book], axis=0)  27.2 us
    dot_general x8, matrix products, body(): backward = jnp.einsum('kce,kcd->ked', joint, at_first, precision=HIGH)  25 us
    dot_general x2, matrix products, accumulate(): jnp.einsum('krc,kre->kce', first_hot, second_hot, preferred_element_type=...  14.7 us
    ppermute x8, waiting for transfers between devices, partner_2(): lax.ppermute(array, axis, [(i, i ^ 1 << bit) for i in range(lax.axis_size...  14.2 us
  transfers between devices with their start and end apart: 9, of which 8 were waited for; matrix products, arithmetic and copies ran while one was open for 1% of the time, Pallas kernels for 0%

commit v1 on v0

v1 whole, which is shorter than its diff:
```python
import functools

import jax
import jax.numpy as jnp
from jax import lax
from jax.experimental import pallas as pl
from jax.experimental.pallas import tpu as pltpu
from jax.sharding import PartitionSpec as P

K = 256
M = 8
ITERS = 8
MESH = pl.DeviceIdType.MESH
HIGH = lax.Precision.HIGHEST
F32 = jnp.float32
BF16 = jnp.bfloat16
NT = (((1,), (1,)), ((), ()))


def vmem():
    return pl.BlockSpec(memory_space=pltpu.VMEM)


def anywhere():
    return pl.BlockSpec(memory_space=pl.ANY)


def split2(value):
    high = value.astype(BF16)
    low = (value - high.astype(F32)).astype(BF16)
    return high, low


def split3(value):
    high = value.astype(BF16)
    rest = value - high.astype(F32)
    middle = rest.astype(BF16)
    low = (rest - middle.astype(F32)).astype(BF16)
    return high, middle, low


def column_groups(groups, width):
    best = 1
    for count in range(1, groups + 1):
        if groups % count == 0 and width % count == 0 and (width // count) % 8 == 0:
            best = count
    return best


def hot_t(row, levels):
    return jnp.where(levels == row, jnp.ones((), BF16), jnp.zeros((), BF16))


def partial_kernel(ncg, nblk, codes_ref, weights_ref, vectors_ref, part_ref):
    rows, width = vectors_ref.shape
    cols = width // ncg
    blk = lax.axis_index("blk")
    parts = jnp.concatenate(split3(vectors_ref[...].T), axis=0)
    levels = lax.broadcasted_iota(jnp.int32, (K, rows), 0).astype(F32).astype(BF16)
    mass = weights_ref[...].astype(BF16)
    for member in range(M // nblk):
        row = codes_ref[pl.ds(nblk * member + blk, 1), :].astype(F32).astype(BF16)
        hot = jnp.where(levels == row, jnp.broadcast_to(mass, (K, rows)), jnp.zeros((), BF16))
        sums = lax.dot_general(parts, hot, NT, preferred_element_type=F32)
        total = sums[:width] + sums[width : 2 * width] + sums[2 * width :]
        for group in range(ncg):
            part_ref[group, member] = total[group * cols : (group + 1) * cols]


def exchange_kernel(n, ncg, gsz, codes_ref, weights_ref, part_ref, codes_out, weights_out, right_out, send_sem, recv_sem, own_sem):
    me = lax.axis_index("dp")
    barrier = pltpu.get_barrier_semaphore()

    def greet(k, carry):
        pl.semaphore_signal(barrier, inc=1, device_id={"dp": lax.rem(me + k, n)}, device_id_type=MESH)
        return carry

    lax.fori_loop(1, n, greet, 0)
    my_part = part_ref.at[lax.rem(me // gsz, ncg), lax.rem(me, gsz)]
    own = [
        pltpu.make_async_copy(codes_ref, codes_out.at[me], own_sem.at[0]),
        pltpu.make_async_copy(weights_ref, weights_out.at[me], own_sem.at[1]),
        pltpu.make_async_copy(my_part, right_out.at[me], own_sem.at[2]),
    ]
    for copy in own:
        copy.start()
    pl.semaphore_wait(barrier, n - 1)

    def copies(k):
        to = lax.rem(me + k, n)
        piece = part_ref.at[lax.rem(to // gsz, ncg), lax.rem(to, gsz)]
        pairs = [(codes_ref, codes_out.at[me]), (weights_ref, weights_out.at[me]), (piece, right_out.at[me])]
        return [
            pltpu.make_async_remote_copy(
                src_ref=source,
                dst_ref=target,
                send_sem=send_sem.at[i, k],
                recv_sem=recv_sem.at[i, k],
                device_id={"dp": to},
                device_id_type=MESH,
            )
            for i, (source, target) in enumerate(pairs)
        ]

    def start(k, carry):
        for copy in copies(k):
            copy.start()
        return carry

    def finish(k, carry):
        for copy in copies(k):
            copy.wait()
        return carry

    lax.fori_loop(1, n, start, 0)
    for copy in own:
        copy.wait()
    lax.fori_loop(1, n, finish, 0)


def gram_kernel(nblk, gsz, codes_ref, weights_ref, gram_ref, count_ref, total_ref):
    step = pl.program_id(0)
    rows = codes_ref.shape[2]
    book = nblk * lax.rem(lax.axis_index("dp"), gsz) + lax.axis_index("blk")

    @pl.when(step == 0)
    def _():
        total_ref[...] = jnp.zeros_like(total_ref)

    levels = lax.broadcasted_iota(jnp.int32, (K, rows), 0).astype(F32).astype(BF16)
    mass = weights_ref[0].astype(BF16)
    mine = codes_ref[0, pl.ds(book, 1), :].astype(F32).astype(BF16)
    weighted = jnp.where(levels == mine, jnp.broadcast_to(mass, (K, rows)), jnp.zeros((), BF16))
    for other in range(M):
        row = codes_ref[0, other : other + 1, :].astype(F32).astype(BF16)
        block = pl.ds(other * K, K)
        total_ref[block, :] += lax.dot_general(hot_t(row, levels), weighted, NT, preferred_element_type=F32)

    @pl.when(step == pl.num_programs(0) - 1)
    def _():
        ones = jnp.ones((8, K), F32)
        for other in range(M):
            block = pl.ds(other * K, K)
            value = total_ref[block, :]
            high, low = split2(value)
            gram_ref[block, :K] = high
            gram_ref[block, K:] = low
            count_ref[other] = lax.dot_general(ones, value, NT, precision=HIGH, preferred_element_type=F32)


def solve_kernel(n, nblk, ncg, gsz, ridge_ref, gram_ref, count_ref, pieces_ref, out_ref,
                 swap, solution, remain, direction, inverse, send_sem, recv_sem, far_send, far_recv, near_send, near_recv):
    cols = pieces_ref.shape[1]
    dp = lax.axis_index("dp")
    blk = lax.axis_index("blk")
    group, member = dp // gsz, lax.rem(dp, gsz)
    book = nblk * member + blk
    bases = (group // ncg) * ncg
    mine = lax.rem(group, ncg)
    half = M // nblk

    def team(k):
        to = lax.rem(book + k, M)
        return {"dp": group * gsz + to // nblk, "blk": lax.rem(to, nblk)}

    def far(k):
        return {"dp": (bases + lax.rem(mine + k, ncg)) * gsz + member, "blk": blk}

    barrier = pltpu.get_barrier_semaphore()
    for k in range(1, M):
        pl.semaphore_signal(barrier, inc=1, device_id=team(k), device_id_type=MESH)
    for k in range(1, ncg):
        pl.semaphore_signal(barrier, inc=1, device_id=far(k), device_id_type=MESH)

    def add(s, total):
        return total + pieces_ref[s]

    right = lax.fori_loop(1, n, add, pieces_ref[0])
    lam = ridge_ref[0] * (jnp.sum(count_ref[0, 0:1, :]) / K)
    for q in range(M):
        inverse[q] = 1.0 / (count_ref[q] + lam)
    pl.semaphore_wait(barrier, M - 1 + ncg - 1)

    def share(slot, value):
        swap[slot, book] = value
        copies = [
            pltpu.make_async_remote_copy(
                src_ref=swap.at[slot, book],
                dst_ref=swap.at[slot, book],
                send_sem=send_sem.at[slot, k],
                recv_sem=recv_sem.at[slot, k],
                device_id=team(k),
                device_id_type=MESH,
            )
            for k in range(1, M)
        ]
        for copy in copies:
            copy.start()
        for copy in copies:
            copy.wait()

    def column(pieces):
        total = pieces[0]
        for piece in pieces[1:]:
            total = total + piece
        return jnp.sum(total, axis=1, keepdims=True)

    share(0, right)
    pieces = []
    for q in range(M):
        r = swap[0, q]
        z = r * inverse[q, 0:1, :]
        remain[q] = r
        direction[q] = z
        solution[q] = jnp.zeros_like(r)
        pieces.append(r * z)

    def iterate(step, inner):
        slot = lax.rem(step + 1, 2)
        product = None
        for q in range(M):
            left = jnp.concatenate(split2(direction[q]), axis=0)
            term = jnp.dot(left, gram_ref[pl.ds(q * K, K), :], preferred_element_type=F32)
            product = term if product is None else product + term
        image = (product[:cols, :K] + product[cols:, :K]) + (product[:cols, K:] + product[cols:, K:])
        share(slot, image)
        pieces = []
        for q in range(M):
            d = direction[q]
            pieces.append(d * (swap[slot, q] + lam * d))
        alpha = inner / column(pieces)
        pieces = []
        for q in range(M):
            d = direction[q]
            r = remain[q] - alpha * (swap[slot, q] + lam * d)
            solution[q] = solution[q] + alpha * d
            remain[q] = r
            pieces.append(r * (r * inverse[q, 0:1, :]))
        fresh = column(pieces)
        beta = fresh / inner
        for q in range(M):
            direction[q] = remain[q] * inverse[q, 0:1, :] + beta * direction[q]
        return fresh

    lax.fori_loop(0, ITERS, iterate, column(pieces))

    for q in range(M):
        out_ref[mine, q] = solution[q]
    part = pl.ds(blk * half, half)
    away = [
        pltpu.make_async_remote_copy(
            src_ref=solution.at[part],
            dst_ref=out_ref.at[mine, part],
            send_sem=far_send.at[k],
            recv_sem=far_recv.at[k],
            device_id=far(k),
            device_id_type=MESH,
        )
        for k in range(1, ncg)
    ]
    for copy in away:
        copy.start()
    relays = []
    for k in range(1, ncg):
        away[k - 1].wait_recv()
        source = lax.rem(mine - k + ncg, ncg)
        for other in range(1, nblk):
            relay = pltpu.make_async_remote_copy(
                src_ref=out_ref.at[source, part],
                dst_ref=out_ref.at[source, part],
                send_sem=near_send.at[k, other],
                recv_sem=near_recv.at[k, other],
                device_id={"dp": dp, "blk": lax.rem(blk + other, nblk)},
                device_id_type=MESH,
            )
            relay.start()
            relays.append(relay)
    for copy in away:
        copy.wait_send()
    for relay in relays:
        relay.wait()


def finish_kernel(codes_ref, weights_ref, vectors_ref, books_ref, book_out, residual_out, sum_out, parts):
    step = pl.program_id(0)
    rows, width = vectors_ref.shape
    ncg = books_ref.shape[0]

    @pl.when(step == 0)
    def _():
        sum_out[...] = jnp.zeros_like(sum_out)
        for q in range(M):
            book = jnp.concatenate([books_ref[c, q] for c in range(ncg)], axis=0).T
            book_out[q] = book
            high, low = split2(book)
            parts[q, :, :width] = high
            parts[q, :, width:] = low

    levels = lax.broadcasted_iota(jnp.int32, (rows, K), 1)
    codes = codes_ref[...]
    total = jnp.zeros((rows, 2 * width), F32)
    for q in range(M):
        hot = jnp.where(levels == codes[:, q : q + 1], 1.0, 0.0).astype(BF16)
        total = total + jnp.dot(hot, parts[q], preferred_element_type=F32)
    residual = vectors_ref[...] - (total[:, :width] + total[:, width:])
    residual_out[...] = residual
    weighted = weights_ref[...] * residual * residual
    sum_out[...] += jnp.broadcast_to(jnp.sum(weighted, keepdims=True), sum_out.shape)


def total_kernel(n, width, part_ref, count_ref, out_ref, gathered, send_sem, recv_sem):
    me = lax.axis_index("dp")
    barrier = pltpu.get_barrier_semaphore()

    def greet(k, carry):
        pl.semaphore_signal(barrier, inc=1, device_id={"dp": lax.rem(me + k, n)}, device_id_type=MESH)
        return carry

    lax.fori_loop(1, n, greet, 0)
    mass = jnp.sum(count_ref[0, 0:1, :]) * width
    pl.semaphore_wait(barrier, n - 1)

    def copy(k):
        return pltpu.make_async_remote_copy(
            src_ref=part_ref,
            dst_ref=gathered.at[me],
            send_sem=send_sem.at[k],
            recv_sem=recv_sem.at[k],
            device_id={"dp": lax.rem(me + k, n)},
            device_id_type=MESH,
        )

    def start(k, carry):
        copy(k).start()
        return carry

    def finish(k, carry):
        copy(k).wait()
        return carry

    lax.fori_loop(1, n, start, 0)
    gathered[me] = part_ref[...]
    lax.fori_loop(1, n, finish, 0)

    def add(s, total):
        return total + gathered[s]

    out_ref[...] = lax.fori_loop(1, n, add, gathered[0]) / mass


def body(vectors, codes, weights, ridge):
    rows, width = vectors.shape
    n, nblk = lax.axis_size("dp"), lax.axis_size("blk")
    gsz = M // nblk
    ncg = column_groups(n // gsz, width)
    cols = width // ncg
    mass = weights.astype(F32)
    codes_t = codes.T
    mass_row = mass[None, :]
    shape = jax.ShapeDtypeStruct

    part = pl.pallas_call(
        functools.partial(partial_kernel, ncg, nblk),
        out_shape=shape((ncg, gsz, cols, K), F32),
        in_specs=[vmem()] * 3,
        out_specs=vmem(),
        name="partial",
    )(codes_t, mass_row, vectors)

    all_codes, all_mass, pieces = pl.pallas_call(
        functools.partial(exchange_kernel, n, ncg, gsz),
        out_shape=(shape((n, M, rows), jnp.int32), shape((n, 1, rows), F32), shape((n, cols, K), F32)),
        in_specs=[vmem()] * 3,
        out_specs=(anywhere(),) * 3,
        scratch_shapes=[
            pltpu.SemaphoreType.DMA((3, n)),
            pltpu.SemaphoreType.DMA((3, n)),
            pltpu.SemaphoreType.DMA((3,)),
        ],
        compiler_params=pltpu.CompilerParams(collective_id=0, has_side_effects=True),
        name="exchange",
    )(codes_t, mass_row, part)

    gram, counts = pl.pallas_call(
        functools.partial(gram_kernel, nblk, gsz),
        grid=(n,),
        out_shape=(shape((M * K, 2 * K), BF16), shape((M, 8, K), F32)),
        in_specs=[
            pl.BlockSpec((1, M, rows), lambda i: (i, 0, 0)),
            pl.BlockSpec((1, 1, rows), lambda i: (i, 0, 0)),
        ],
        out_specs=(
            pl.BlockSpec((M * K, 2 * K), lambda i: (0, 0)),
            pl.BlockSpec((M, 8, K), lambda i: (0, 0, 0)),
        ),
        scratch_shapes=[pltpu.VMEM((M * K, K), F32)],
        compiler_params=pltpu.CompilerParams(dimension_semantics=("arbitrary",)),
        name="gram",
    )(all_codes, all_mass)

    state = pltpu.VMEM((M, cols, K), F32)
    dma = pltpu.SemaphoreType.DMA
    books = pl.pallas_call(
        functools.partial(solve_kernel, n, nblk, ncg, gsz),
        out_shape=shape((ncg, M, cols, K), F32),
        in_specs=[pl.BlockSpec(memory_space=pltpu.SMEM)] + [vmem()] * 3,
        out_specs=vmem(),
        scratch_shapes=[
            pltpu.VMEM((2, M, cols, K), F32), state, state, state, pltpu.VMEM((M, 8, K), F32),
            dma((2, M)), dma((2, M)), dma((ncg,)), dma((ncg,)), dma((ncg, nblk)), dma((ncg, nblk)),
        ],
        compiler_params=pltpu.CompilerParams(collective_id=1, has_side_effects=True),
        name="solve",
    )(ridge, gram, counts, pieces)

    step_rows = min(256, rows)
    codebooks, residual, local = pl.pallas_call(
        finish_kernel,
        grid=(rows // step_rows,),
        out_shape=(shape((M, K, width), F32), shape((rows, width), F32), shape((8, 128), F32)),
        in_specs=[
            pl.BlockSpec((step_rows, M), lambda i: (i, 0)),
            pl.BlockSpec((step_rows, 1), lambda i: (i, 0)),
            pl.BlockSpec((step_rows, width), lambda i: (i, 0)),
            pl.BlockSpec((ncg, M, cols, K), lambda i: (0, 0, 0, 0)),
        ],
        out_specs=(
            pl.BlockSpec((M, K, width), lambda i: (0, 0, 0)),
            pl.BlockSpec((step_rows, width), lambda i: (i, 0)),
            pl.BlockSpec((8, 128), lambda i: (0, 0)),
        ),
        scratch_shapes=[pltpu.VMEM((M, K, 2 * width), BF16)],
        compiler_params=pltpu.CompilerParams(dimension_semantics=("arbitrary",)),
        name="finish",
    )(codes, mass[:, None], vectors, books)

    distortion = pl.pallas_call(
        functools.partial(total_kernel, n, width),
        out_shape=shape((8, 128), F32),
        in_specs=[vmem()] * 2,
        out_specs=vmem(),
        scratch_shapes=[pltpu.VMEM((n, 8, 128), F32), dma((n,)), dma((n,))],
        compiler_params=pltpu.CompilerParams(collective_id=2, has_side_effects=True),
        name="total",
    )(local, counts)
    return (codebooks, residual, distortion[0, 0])


def solution(mesh):
    return jax.shard_map(
        body,
        mesh=mesh,
        in_specs=(P("dp", None), P("dp", None), P("dp"), P()),
        out_specs=(P(), P("dp", None), P()),
        check_vma=False,
    )
```

time: 448 us -> 144 us (0.32)
  waiting for transfers between devices: 134 us -> 0 us
  Pallas kernels: 0 us -> 132 us
  matrix products: 118 us -> 0 us
  blocking collectives: 90.7 us -> 0 us
  local copies, waits for them, and re-layouts: 46.5 us -> 8.59 us
  other arithmetic: 32.8 us -> 1.28 us
  between operations: 19 us -> 1.33 us
    pallas_call x0 -> x6, Pallas kernels: none -> 132 us  [the longest x1 63.6 us: body(): pl.pallas_call(functools.partial(solve_kernel, n, nblk, ncg, gsz), out_sh...]
    psum x1 -> x0, waiting for transfers between devices: 120 us -> none  [body(): lax.psum((joint, right_part, count_part), 'dp')]
    dot_general x52 -> x0, matrix products: 118 us -> none  [the longest x8 36.4 us: body(): forward = jnp.einsum('kce,ked->kcd', joint, at_second, precision=HIGH)]
    psum x2 -> x0, blocking collectives: 86.1 us -> none  [the longest x1 45.8 us: body(): lax.psum((joint, right_part, count_part), 'dp')]
    gather x12 -> x0, local copies, waits for them, and re-layouts: 37.8 us -> none  [the longest x8 27.2 us: body(): recon = recon + jnp.take(solution[book], codes[:, book], axis=0)]
    reduce_sum x19 -> x0, other arithmetic: 24.5 us -> none  [the longest x7 11.4 us: body(): fresh = jnp.sum(remain * scaled, axis=(0, 1))]
    ppermute x8 -> x0, waiting for transfers between devices: 14.2 us -> none  [partner_2(): lax.ppermute(array, axis, [(i, i ^ 1 << bit) for i in range(lax.axis_size...]
    all_gather x2 -> x0, blocking collectives: 4.55 us -> none  [the longest x1 2.74 us: body(): lax.all_gather(right_part, 'blk', axis=0, tiled=True)]
  transfers between devices with their start and end apart: 9 -> 0, of which waited for: 8 -> 0; matrix products, arithmetic and copies ran while one was open for 1% -> 0% of each run, Pallas kernels for 0% -> 0%
where the time goes in v1:
time: 144 us; the launch traced here: 143 us
  Pallas kernels  132 us (92%)
  local copies, waits for them, and re-layouts  8.59 us (6%)
    pallas_call x1, Pallas kernels, body(): pl.pallas_call(functools.partial(solve_kernel, n, nblk, ncg, gsz), out_sh...  63.6 us
    pallas_call x1, Pallas kernels, body(): pl.pallas_call(functools.partial(gram_kernel, nblk, gsz), grid=(n,), out_...  25.1 us
    pallas_call x1, Pallas kernels, body(): pl.pallas_call(functools.partial(exchange_kernel, n, ncg, gsz), out_shape...  24.7 us
    pallas_call x1, Pallas kernels, body(): pl.pallas_call(functools.partial(total_kernel, n, width), out_shape=shape...  10.1 us
    unnamed x10, local copies, waits for them, and re-layouts  6.38 us
    pallas_call x1, Pallas kernels, body(): pl.pallas_call(finish_kernel, grid=(rows // step_rows,), out_shape=(shape...  5.94 us

profile of v1, /device:TPU:0, one launch (start us, length us, event | category | flops | bytes accessed | tf_op | source)
XLA Modules:
  0.0 143.3 jit_solution(3573507084133172664)
XLA Ops:
  0.6 1.3 convert_element_type.3
  1.9 2.0 %copy.15.vectors_ref = f32[1024,96]{1,0:T(8,128)} copy(f32[1024,96]{0,1:T(8,128)} %param.4) | data formatting | bytes 786432 | tf_op args[0]
  3.9 2.7 %partial.1.part_ref = f32[4,4,24,256]{3,2,1,0:T(8,128)} custom-call(s32[8,1024]{1,0:T(8,128)} %bitcast.4, f32[1,1024]{1,0:T(1,128)} %bitcast.6, f32[1024,96]{1,0:T(8,128)} %copy.15.vectors_ref), custom_call_target="tpu_custom_call" | custom-call | tf_op jit(solution)/shard_map/partial/pallas_call | solution.py:362
  6.6 0.0 copy-start.2
  6.6 24.7 %exchange.1 = (s32[16,8,1024]{2,1,0:T(8,128)}, f32[16,1,1024]{2,1,0:T(1,128)}, f32[16,24,256]{2,1,0:T(8,128)}) custom-call(s32[8,1024]{1,0:T(8,128)} %bitcast.5, f32[1,1024]{1,0:T(1,128)} %bitcast.7, f32[4,4,24,256]{3,2,1,0:T(8,128)} %partial.1.part_ref), custom_call_target="tpu_custom_call" | custom-call | tf_op jit(solution)/shard_map/exchange/pallas_call | solution.py:370
  31.3 0.0 copy-start.1
  31.3 25.1 %gram.1 = (bf16[2048,512]{1,0:T(8,128)(2,1)}, f32[8,8,256]{2,1,0:T(8,128)}) custom-call(s32[16,8,1024]{2,1,0:T(8,128)} %get-tuple-element.11.codes_ref, f32[16,1,1024]{2,1,0:T(1,128)} %get-tuple-element.12.weights_ref), custom_call_target="tpu_custom_call" | custom-call | tf_op jit(solution)/shard_map/gram/pallas_call | solution.py:384
  57.1 63.6 %solve.1.books_ref = f32[4,8,24,256]{3,2,1,0:T(8,128)} custom-call(f32[1]{0:T(128)S(6)} %copy.18.ridge_ref, bf16[2048,512]{1,0:T(8,128)(2,1)} %get-tuple-element.13.gram_ref, f32[8,8,256]{2,1,0:T(8,128)} %get-tuple-element.14.count_ref, f32[16,24,256]{2,1,0:T(8,128)} %get-tuple-element.15.pieces_ref), custom_call_target="tpu_custom_call" | custom-call | tf_op jit(solution)/shard_map/solve/pallas_call | solution.py:403
  120.7 0.0 copy-done.2
  120.7 1.0 copy.14.weights_ref
  121.7 0.0 copy-done.1
  121.7 1.0 copy.13.codes_ref
  122.7 5.9 %finish.1 = (f32[8,256,96]{2,1,0:T(8,128)}, f32[1024,96]{1,0:T(8,128)}, f32[8,128]{1,0:T(8,128)}) custom-call(s32[1024,8]{1,0:T(8,128)} %copy.13.codes_ref, f32[1024,1]{1,0:T(8,128)} %copy.14.weights_ref, f32[1024,96]{1,0:T(8,128)} %copy.15.vectors_ref, f32[4,8,24,256]{3,2,1,0:T(8,128)} %solve.1.books_ref), custom_call_target="tpu_custom_call" | custom-call | tf_op jit(solution)/shard_map/finish/pallas_call | solution.py:417
  128.6 0.0 copy-start
  128.6 10.1 %total.1 = f32[8,128]{1,0:T(8,128)} custom-call(f32[8,128]{1,0:T(8,128)} %get-tuple-element.18.part_ref, f32[8,8,256]{2,1,0:T(8,128)} %get-tuple-element.14.count_ref), custom_call_target="tpu_custom_call" | custom-call | tf_op jit(solution)/shard_map/total/pallas_call | solution.py:437
  138.8 1.2 slice.3
  140.0 2.4 %copy.16 = f32[8,256,96]{1,2,0:T(8,128)} copy(f32[8,256,96]{2,1,0:T(8,128)} %get-tuple-element.22) | data formatting | bytes 1572864
  142.4 0.0 copy-done
  142.4 0.9 copy.17
Async XLA Ops:
  6.6 114.1 %copy-start.2 = (f32[1024]{0:T(1024)S(1)}, f32[1024]{0:T(1024)}, u32[]{:S(2)}) copy-start(f32[1024]{0:T(1024)} %convert_element_type.3) | copy-start | bytes 12292
  31.3 90.4 %copy-start.1 = (s32[1024,8]{0,1:T(8,128)S(1)}, s32[1024,8]{0,1:T(8,128)}, u32[]{:S(2)}) copy-start(s32[1024,8]{0,1:T(8,128)} %param.5) | copy-start | bytes 98308
  128.6 13.8 %copy-start = (f32[1024,96]{1,0:T(8,128)S(1)}, f32[1024,96]{1,0:T(8,128)}, u32[]{:S(2)}) copy-start(f32[1024,96]{1,0:T(8,128)} %get-tuple-element.23) | copy-start | bytes 1179652

commit v2 on v0

v2 whole, which is shorter than its diff:
```python
import functools

import jax
import jax.numpy as jnp
from jax import lax
from jax.experimental import pallas as pl
from jax.experimental.pallas import tpu as pltpu
from jax.sharding import PartitionSpec as P

K = 256
M = 8
ITERS = 8
MESH = pl.DeviceIdType.MESH
HIGH = lax.Precision.HIGHEST
F32 = jnp.float32
BF16 = jnp.bfloat16
NT = (((1,), (1,)), ((), ()))


def vmem():
    return pl.BlockSpec(memory_space=pltpu.VMEM)


def split2(value):
    high = value.astype(BF16)
    low = (value - high.astype(F32)).astype(BF16)
    return high, low


def split3(value):
    high = value.astype(BF16)
    rest = value - high.astype(F32)
    middle = rest.astype(BF16)
    low = (rest - middle.astype(F32)).astype(BF16)
    return high, middle, low


def column_groups(groups, width):
    best = 1
    for count in range(1, groups + 1):
        if groups % count == 0 and width % count == 0 and (width // count) % 8 == 0:
            best = count
    return best


def hot_t(row, levels):
    return jnp.where(levels == row, jnp.ones((), BF16), jnp.zeros((), BF16))


def flip(value, mask, size):
    total, digit = 0, 1
    while digit < size:
        total = total + digit * lax.rem(value // digit + mask // digit % 2, 2)
        digit *= 2
    return total


def column(pieces):
    total = pieces[0]
    for piece in pieces[1:]:
        total = total + piece
    return jnp.sum(total, axis=1, keepdims=True)


def kernel(n, nblk, ncg, ridge_ref, codes_ref, mass_ref, vectors_ref, book_out, residual_out, sum_out,
           codes_all, mass_all, part, pieces, gram, halves, swap, solution, remain, direction, inverse,
           books, parts, gathered, send_sem, recv_sem, swap_send, swap_recv, far_send, far_recv,
           near_send, near_recv, sum_send, sum_recv):
    width, rows = vectors_ref.shape
    gsz = M // nblk
    cols = width // ncg
    me = lax.axis_index("dp")
    blk = lax.axis_index("blk")
    group, member = me // gsz, lax.rem(me, gsz)
    book = nblk * member + blk
    mine = lax.rem(group, ncg)
    bases = group - mine
    half = M // nblk
    peers = [(dm, db) for dm in range(gsz - 1, -1, -1) for db in range(nblk - 1, -1, -1) if (dm, db) != (0, 0)]

    def chip(k):
        return {"dp": lax.rem(me + k, n)}

    def team(dm, db):
        return {"dp": group * gsz + flip(member, dm, gsz), "blk": lax.rem(blk + db, nblk)}

    def far(k):
        return {"dp": (bases + lax.rem(mine + k, ncg)) * gsz + member, "blk": blk}

    def remote(source, target, send, recv, to):
        return pltpu.make_async_remote_copy(
            src_ref=source, dst_ref=target, send_sem=send, recv_sem=recv, device_id=to, device_id_type=MESH
        )

    def loop(function):
        def step(k, carry):
            function(k)
            return carry

        lax.fori_loop(1, n, step, 0)

    barrier = pltpu.get_barrier_semaphore()
    loop(lambda k: pl.semaphore_signal(barrier, inc=1, device_id=chip(k), device_id_type=MESH))
    others = [(dm, db) for dm, db in peers if db]
    for dm, db in others:
        pl.semaphore_signal(barrier, inc=1, device_id=team(dm, db), device_id_type=MESH)

    triple = jnp.concatenate(split3(vectors_ref[...]), axis=0)
    levels = lax.broadcasted_iota(jnp.int32, (K, rows), 0).astype(F32).astype(BF16)

    def spread(row, mass):
        return jnp.where(levels == row.astype(F32).astype(BF16), jnp.broadcast_to(mass, (K, rows)), jnp.zeros((), BF16))

    for m in range(gsz):
        hot = spread(codes_ref[pl.ds(nblk * m + blk, 1), :], mass_ref[...].astype(BF16))
        sums = lax.dot_general(triple, hot, NT, preferred_element_type=F32)
        total = sums[:width] + sums[width : 2 * width] + sums[2 * width :]
        for c in range(ncg):
            part[c, m] = total[c * cols : (c + 1) * cols]
    pl.semaphore_wait(barrier, n - 1 + len(others))

    def codes_copy(k):
        return remote(codes_ref, codes_all.at[me], send_sem.at[0, k], recv_sem.at[0, k], chip(k))

    def mass_copy(k):
        return remote(mass_ref, mass_all.at[me], send_sem.at[1, k], recv_sem.at[1, k], chip(k))

    def piece_copy(k):
        to = lax.rem(me + k, n)
        piece = part.at[lax.rem(to // gsz, ncg), lax.rem(to, gsz)]
        return remote(piece, pieces.at[me], send_sem.at[2, k], recv_sem.at[2, k], chip(k))

    def send_codes(k):
        codes_copy(k).start()
        mass_copy(k).start()

    loop(send_codes)
    loop(lambda k: piece_copy(k).start())

    codes_all[me] = codes_ref[...]
    mass_all[me] = mass_ref[...]
    pieces[me] = part[mine, member]
    gram[...] = jnp.zeros_like(gram)

    def block(q):
        return pl.ds(pl.multiple_of(q * K, K), K)

    def accumulate(source):
        weighted = spread(codes_all[source, pl.ds(book, 1), :], mass_all[source].astype(BF16))
        for j in range(1, M):
            other = lax.rem(book + j, M)
            hot = spread(codes_all[source, pl.ds(other, 1), :], jnp.ones((1, 1), BF16))
            gram[block(other), :] += lax.dot_general(hot, weighted, NT, preferred_element_type=F32)

    accumulate(me)

    def arrive(k):
        codes_copy(k).wait_recv()
        mass_copy(k).wait_recv()
        accumulate(lax.rem(me - k + n, n))

    loop(arrive)

    square = (K, K)
    own = jnp.sum(gram[block(lax.rem(book + 1, M)), :], axis=0, keepdims=True)
    diagonal = lax.broadcasted_iota(jnp.int32, square, 0) == lax.broadcasted_iota(jnp.int32, square, 1)
    gram[block(book), :] = jnp.where(diagonal, jnp.broadcast_to(own, square), 0.0)
    ones = jnp.ones((8, K), F32)
    for q in range(M):
        value = gram[block(q), :]
        high, low = split2(value)
        halves[block(q), :K] = high
        halves[block(q), K:] = low
        inverse[q] = lax.dot_general(ones, value, NT, precision=HIGH, preferred_element_type=F32)
    whole = jnp.sum(inverse[0, 0:1, :])
    lam = ridge_ref[0] * (whole / K)
    for q in range(M):
        inverse[q] = 1.0 / (inverse[q] + lam)

    loop(lambda k: piece_copy(k).wait_recv())
    right = lax.fori_loop(1, n, lambda s, total: total + pieces[s], pieces[0])

    def share(slot, value):
        swap[slot, book] = value
        here = swap.at[slot, book]
        copies = [
            remote(here, here, swap_send.at[slot, i], swap_recv.at[slot, i], team(dm, db))
            for i, (dm, db) in enumerate(peers)
        ]
        for copy in copies:
            copy.start()
        for copy in copies:
            copy.wait()

    share(0, right)
    terms = []
    for q in range(M):
        r = swap[0, q]
        z = r * inverse[q, 0:1, :]
        remain[q] = r
        direction[q] = z
        solution[q] = jnp.zeros_like(r)
        terms.append(r * z)

    def iterate(step, inner):
        slot = lax.rem(step + 1, 2)
        product = None
        for q in range(M):
            left = jnp.concatenate(split2(direction[q]), axis=0)
            term = jnp.dot(left, halves[pl.ds(q * K, K), :], preferred_element_type=F32)
            product = term if product is None else product + term
        image = (product[:cols, :K] + product[cols:, :K]) + (product[:cols, K:] + product[cols:, K:])
        share(slot, image)
        terms = []
        for q in range(M):
            d = direction[q]
            terms.append(d * (swap[slot, q] + lam * d))
        alpha = inner / column(terms)
        terms = []
        for q in range(M):
            d = direction[q]
            r = remain[q] - alpha * (swap[slot, q] + lam * d)
            solution[q] = solution[q] + alpha * d
            remain[q] = r
            terms.append(r * (r * inverse[q, 0:1, :]))
        fresh = column(terms)
        beta = fresh / inner
        for q in range(M):
            direction[q] = remain[q] * inverse[q, 0:1, :] + beta * direction[q]
        return fresh

    lax.fori_loop(0, ITERS, iterate, column(terms))

    span = pl.ds(blk * half, half)
    away = [
        remote(solution.at[span], books.at[mine, span], far_send.at[k], far_recv.at[k], far(k)) for k in range(1, ncg)
    ]
    for copy in away:
        copy.start()
    for q in range(M):
        books[mine, q] = solution[q]
    relays = []
    for k in range(1, ncg):
        away[k - 1].wait_recv()
        there = books.at[lax.rem(mine - k + ncg, ncg), span]
        for db in range(1, nblk):
            relay = remote(there, there, near_send.at[k, db], near_recv.at[k, db], team(0, db))
            relay.start()
            relays.append(relay)
    for relay in relays:
        relay.wait()

    for q in range(M):
        value = jnp.concatenate([books[c, q] for c in range(ncg)], axis=0)
        book_out[q] = value
        high, low = split2(value)
        parts[q, :width, :] = high
        parts[q, width:, :] = low

    size = min(256, rows)
    short = lax.broadcasted_iota(jnp.int32, (K, size), 0).astype(F32).astype(BF16)

    def rebuild(turn, total):
        at = pl.ds(pl.multiple_of(turn * size, size), size)
        value = jnp.zeros((2 * width, size), F32)
        for q in range(M):
            row = codes_ref[q : q + 1, at].astype(F32).astype(BF16)
            value = value + jnp.dot(parts[q], hot_t(row, short), preferred_element_type=F32)
        residual = vectors_ref[:, at] - (value[:width] + value[width:])
        residual_out[:, at] = residual
        return total + mass_ref[:, at] * (residual * residual)

    total = lax.fori_loop(0, rows // size, rebuild, jnp.zeros((width, size), F32))
    gathered[me] = jnp.broadcast_to(jnp.sum(total, keepdims=True), (8, 128))

    def sum_copy(k):
        return remote(gathered.at[me], gathered.at[me], sum_send.at[k], sum_recv.at[k], chip(k))

    loop(lambda k: sum_copy(k).start())
    for copy in away:
        copy.wait_send()

    def drain(k):
        codes_copy(k).wait_send()
        mass_copy(k).wait_send()
        piece_copy(k).wait_send()

    loop(drain)
    loop(lambda k: sum_copy(k).wait())
    final = lax.fori_loop(1, n, lambda s, value: value + gathered[s], gathered[0])
    sum_out[...] = final / (whole * width)


def body(vectors, codes, weights, ridge):
    rows, width = vectors.shape
    n, nblk = lax.axis_size("dp"), lax.axis_size("blk")
    gsz = M // nblk
    ncg = column_groups(n // gsz, width)
    cols = width // ncg
    shape = jax.ShapeDtypeStruct
    dma = pltpu.SemaphoreType.DMA
    state = pltpu.VMEM((M, cols, K), F32)
    books, residual, distortion = pl.pallas_call(
        functools.partial(kernel, n, nblk, ncg),
        out_shape=(shape((M, width, K), F32), shape((width, rows), F32), shape((8, 128), F32)),
        in_specs=[pl.BlockSpec(memory_space=pltpu.SMEM)] + [vmem()] * 3,
        out_specs=(vmem(),) * 3,
        scratch_shapes=[
            pltpu.VMEM((n, M, rows), jnp.int32),
            pltpu.VMEM((n, 1, rows), F32),
            pltpu.VMEM((ncg, gsz, cols, K), F32),
            pltpu.VMEM((n, cols, K), F32),
            pltpu.VMEM((M * K, K), F32),
            pltpu.VMEM((M * K, 2 * K), BF16),
            pltpu.VMEM((2, M, cols, K), F32),
            state,
            state,
            state,
            pltpu.VMEM((M, 8, K), F32),
            pltpu.VMEM((ncg, M, cols, K), F32),
            pltpu.VMEM((M, 2 * width, K), BF16),
            pltpu.VMEM((n, 8, 128), F32),
            dma((3, n)),
            dma((3, n)),
            dma((2, M)),
            dma((2, M)),
            dma((ncg,)),
            dma((ncg,)),
            dma((ncg, nblk)),
            dma((ncg, nblk)),
            dma((n,)),
            dma((n,)),
        ],
        compiler_params=pltpu.CompilerParams(collective_id=0, has_side_effects=True),
        name="update",
    )(ridge, codes.T, weights.astype(F32)[None, :], vectors.T)
    return (books.transpose(0, 2, 1), residual.T, distortion[0, 0])


def solution(mesh):
    return jax.shard_map(
        body,
        mesh=mesh,
        in_specs=(P("dp", None), P("dp", None), P("dp"), P()),
        out_specs=(P(), P("dp", None), P()),
        check_vma=False,
    )
```

time: 448 us -> 103 us (0.23); the launches traced: 443 us -> 103 us
  waiting for transfers between devices: 134 us -> 0 us
  matrix products: 118 us -> 0 us
  Pallas kernels: 0 us -> 96.3 us
  blocking collectives: 90.7 us -> 0 us
  local copies, waits for them, and re-layouts: 46.5 us -> 4.73 us
  other arithmetic: 32.8 us -> 0.59 us
  between operations: 19 us -> 1.3 us
    psum x1 -> x0, waiting for transfers between devices: 120 us -> none  [body(): lax.psum((joint, right_part, count_part), 'dp')]
    dot_general x52 -> x0, matrix products: 118 us -> none  [the longest x8 36.4 us: body(): forward = jnp.einsum('kce,ked->kcd', joint, at_second, precision=HIGH)]
    pallas_call x0 -> x1, Pallas kernels: none -> 96.3 us  [body(): pl.pallas_call(functools.partial(kernel, n, nblk, ncg), out_shape=(shape(...]
    psum x2 -> x0, blocking collectives: 86.1 us -> none  [the longest x1 45.8 us: body(): lax.psum((joint, right_part, count_part), 'dp')]
    gather x12 -> x0, local copies, waits for them, and re-layouts: 37.8 us -> none  [the longest x8 27.2 us: body(): recon = recon + jnp.take(solution[book], codes[:, book], axis=0)]
    reduce_sum x19 -> x0, other arithmetic: 24.5 us -> none  [the longest x7 11.4 us: body(): fresh = jnp.sum(remain * scaled, axis=(0, 1))]
    ppermute x8 -> x0, waiting for transfers between devices: 14.2 us -> none  [partner_2(): lax.ppermute(array, axis, [(i, i ^ 1 << bit) for i in range(lax.axis_size...]
    all_gather x2 -> x0, blocking collectives: 4.55 us -> none  [the longest x1 2.74 us: body(): lax.all_gather(right_part, 'blk', axis=0, tiled=True)]
  transfers between devices with their start and end apart: 9 -> 0, of which waited for: 8 -> 0; matrix products, arithmetic and copies ran while one was open for 1% -> 0% of each run, Pallas kernels for 0% -> 0%
where the time goes in v2:
time: 103 us
  Pallas kernels  96.3 us (93%)
  local copies, waits for them, and re-layouts  4.73 us (5%)
  between operations  1.3 us (1%)
    pallas_call x1, Pallas kernels, body(): pl.pallas_call(functools.partial(kernel, n, nblk, ncg), out_shape=(shape(...  96.3 us
    unnamed x6, local copies, waits for them, and re-layouts  3.54 us

profile of v2, /device:TPU:0, one launch (start us, length us, event | category | flops | bytes accessed | tf_op | source)
XLA Modules:
  0.0 102.9 jit_solution(17406001675053801768)
XLA Ops:
  1.3 0.0 copy-start.1
  1.3 0.7 copy-done.1
  2.0 0.6 broadcast_in_dim.7
  2.6 96.3 %update.1 = (f32[8,96,256]{2,1,0:T(8,128)}, f32[96,1024]{1,0:T(8,128)}, f32[8,128]{1,0:T(8,128)}) custom-call(f32[1]{0:T(128)S(6)} %copy.9.ridge_ref, s32[8,1024]{1,0:T(8,128)} %bitcast.9, f32[1,1024]{1,0:T(1,128)} %bitcast.10, f32[96,1024]{1,0:T(8,128)} %bitcast.8), custom_call_target="tpu_custom_call" | custom-call | tf_op jit(solution)/shard_map/update/pallas_call | solution.py:303
  98.9 1.2 %slice.3 = f32[1,1]{1,0:T(1,128)} slice(f32[8,128]{1,0:T(8,128)} %get-tuple-element.8), slice={[0:1], [0:1]} | slice | bytes 8 | tf_op jit(solution)/shard_map/slice | solution.py:337
  100.1 0.0 copy-start
  100.1 2.1 %copy.10 = f32[8,256,96]{1,2,0:T(8,128)} copy(f32[8,256,96]{1,2,0:T(8,128)} %bitcast.6) | data formatting | bytes 1572864
  102.2 0.0 copy-done
  102.2 0.7 copy.11
Async XLA Ops:
  1.3 0.7 copy-start.1
  100.1 2.1 %copy-start = (f32[96,1024]{1,0:T(8,128)S(1)}, f32[96,1024]{1,0:T(8,128)}, u32[]{:S(2)}) copy-start(f32[96,1024]{1,0:T(8,128)} %get-tuple-element.7) | copy-start | bytes 1179652

commit v3 on v2

--- a/solution.py
+++ b/solution.py
@@ -135,7 +135,6 @@
         mass_copy(k).start()
 
     loop(send_codes)
-    loop(lambda k: piece_copy(k).start())
 
     codes_all[me] = codes_ref[...]
     mass_all[me] = mass_ref[...]
@@ -157,6 +156,7 @@
     def arrive(k):
         codes_copy(k).wait_recv()
         mass_copy(k).wait_recv()
+        piece_copy(k).start()
         accumulate(lax.rem(me - k + n, n))
 
     loop(arrive)
@@ -180,56 +180,84 @@
     loop(lambda k: piece_copy(k).wait_recv())
     right = lax.fori_loop(1, n, lambda s, total: total + pieces[s], pieces[0])
 
-    def share(slot, value):
-        swap[slot, book] = value
-        here = swap.at[slot, book]
-        copies = [
-            remote(here, here, swap_send.at[slot, i], swap_recv.at[slot, i], team(dm, db))
-            for i, (dm, db) in enumerate(peers)
+    cut = (cols // 8 + 1) // 2 * 8
+    streams = [(i, pl.ds(first, last - first), last - first) for i, (first, last) in enumerate([(0, cut), (cut, cols)]) if last > first]
+
+    def copies(stream, slot):
+        i, span, _ = stream
+        here = swap.at[slot, book, span]
+        return [
+            remote(here, here, swap_send.at[slot, i, j], swap_recv.at[slot, i, j], team(dm, db))
+            for j, (dm, db) in enumerate(peers)
         ]
-        for copy in copies:
+
+    def send(stream, slot, value):
+        swap[slot, book, stream[1]] = value
+        for copy in copies(stream, slot):
             copy.start()
-        for copy in copies:
+
+    def receive(stream, slot):
+        for copy in copies(stream, slot):
             copy.wait()
 
-    share(0, right)
-    terms = []
-    for q in range(M):
-        r = swap[0, q]
-        z = r * inverse[q, 0:1, :]
-        remain[q] = r
-        direction[q] = z
-        solution[q] = jnp.zeros_like(r)
-        terms.append(r * z)
-
-    def iterate(step, inner):
-        slot = lax.rem(step + 1, 2)
+    def apply(stream):
+        _, span, size = stream
         product = None
         for q in range(M):
-            left = jnp.concatenate(split2(direction[q]), axis=0)
+            left = jnp.concatenate(split2(direction[q, span]), axis=0)
             term = jnp.dot(left, halves[pl.ds(q * K, K), :], preferred_element_type=F32)
             product = term if product is None else product + term
-        image = (product[:cols, :K] + product[cols:, :K]) + (product[:cols, K:] + product[cols:, K:])
-        share(slot, image)
+        return (product[:size, :K] + product[size:, :K]) + (product[:size, K:] + product[size:, K:])
+
+    def begin(stream):
+        _, span, _ = stream
+        receive(stream, 0)
         terms = []
         for q in range(M):
-            d = direction[q]
-            terms.append(d * (swap[slot, q] + lam * d))
+            r = swap[0, q, span]
+            z = r * inverse[q, 0:1, :]
+            remain[q, span] = r
+            direction[q, span] = z
+            solution[q, span] = jnp.zeros_like(r)
+            terms.append(r * z)
+        send(stream, 1, apply(stream))
+        return column(terms)
+
+    def advance(stream, slot, inner):
+        _, span, _ = stream
+        receive(stream, slot)
+        terms = []
+        for q in range(M):
+            d = direction[q, span]
+            terms.append(d * (swap[slot, q, span] + lam * d))
         alpha = inner / column(terms)
         terms = []
         for q in range(M):
-            d = direction[q]
-            r = remain[q] - alpha * (swap[slot, q] + lam * d)
-            solution[q] = solution[q] + alpha * d
-            remain[q] = r
+            d = direction[q, span]
+            r = remain[q, span] - alpha * (swap[slot, q, span] + lam * d)
+            solution[q, span] = solution[q, span] + alpha * d
+            remain[q, span] = r
             terms.append(r * (r * inverse[q, 0:1, :]))
         fresh = column(terms)
         beta = fresh / inner
         for q in range(M):
-            direction[q] = remain[q] * inverse[q, 0:1, :] + beta * direction[q]
+            direction[q, span] = remain[q, span] * inverse[q, 0:1, :] + beta * direction[q, span]
         return fresh
 
-    lax.fori_loop(0, ITERS, iterate, column(terms))
+    def iterate(step, inners):
+        slot = lax.rem(step, 2)
+        results = []
+        for stream, inner in zip(streams, inners):
+            results.append(advance(stream, slot, inner))
+            send(stream, 1 - slot, apply(stream))
+        return tuple(results)
+
+    for stream in streams:
+        first = stream[1].start
+        send(stream, 0, right[first : first + stream[2]])
+    inners = lax.fori_loop(1, ITERS, iterate, tuple(begin(stream) for stream in streams))
+    for stream, inner in zip(streams, inners):
+        advance(stream, ITERS % 2, inner)
 
     span = pl.ds(blk * half, half)
     away = [
@@ -322,8 +350,8 @@
             pltpu.VMEM((n, 8, 128), F32),
             dma((3, n)),
             dma((3, n)),
-            dma((2, M)),
-            dma((2, M)),
+            dma((2, 2, M)),
+            dma((2, 2, M)),
             dma((ncg,)),
             dma((ncg,)),
             dma((ncg, nblk)),

time: 103 us -> 103 us (level)
  no operation moved by 1% of the time
where the time goes in v3:
time: 103 us
  Pallas kernels  96.1 us (93%)
  local copies, waits for them, and re-layouts  4.73 us (5%)
  between operations  1.3 us (1%)
    pallas_call x1, Pallas kernels, body(): pl.pallas_call(functools.partial(kernel, n, nblk, ncg), out_shape=(shape(...  96.1 us
    unnamed x6, local copies, waits for them, and re-layouts  3.54 us

profile of v3, /device:TPU:0, one launch (start us, length us, event | category | flops | bytes accessed | tf_op | source)
XLA Modules:
  0.0 102.7 jit_solution(14806983425982617021)
XLA Ops:
  1.3 0.0 copy-start.1
  1.3 0.7 copy-done.1
  2.0 0.6 broadcast_in_dim.7
  2.6 96.1 %update.1 = (f32[8,96,256]{2,1,0:T(8,128)}, f32[96,1024]{1,0:T(8,128)}, f32[8,128]{1,0:T(8,128)}) custom-call(f32[1]{0:T(128)S(6)} %copy.9.ridge_ref, s32[8,1024]{1,0:T(8,128)} %bitcast.9, f32[1,1024]{1,0:T(1,128)} %bitcast.10, f32[96,1024]{1,0:T(8,128)} %bitcast.8), custom_call_target="tpu_custom_call" | custom-call | tf_op jit(solution)/shard_map/update/pallas_call | solution.py:331
  98.7 1.2 %slice.3 = f32[1,1]{1,0:T(1,128)} slice(f32[8,128]{1,0:T(8,128)} %get-tuple-element.8), slice={[0:1], [0:1]} | slice | bytes 8 | tf_op jit(solution)/shard_map/slice | solution.py:365
  99.8 0.0 copy-start
  99.8 2.1 %copy.10 = f32[8,256,96]{1,2,0:T(8,128)} copy(f32[8,256,96]{1,2,0:T(8,128)} %bitcast.6) | data formatting | bytes 1572864
  102.0 0.0 copy-done
  102.0 0.7 copy.11
Async XLA Ops:
  1.3 0.7 copy-start.1
  99.8 2.1 %copy-start = (f32[96,1024]{1,0:T(8,128)S(1)}, f32[96,1024]{1,0:T(8,128)}, u32[]{:S(2)}) copy-start(f32[96,1024]{1,0:T(8,128)} %get-tuple-element.7) | copy-start | bytes 1179652

commit v4 on v3

--- a/solution.py
+++ b/solution.py
@@ -65,7 +65,7 @@
 def kernel(n, nblk, ncg, ridge_ref, codes_ref, mass_ref, vectors_ref, book_out, residual_out, sum_out,
            codes_all, mass_all, part, pieces, gram, halves, swap, solution, remain, direction, inverse,
            books, parts, gathered, send_sem, recv_sem, swap_send, swap_recv, far_send, far_recv,
-           near_send, near_recv, sum_send, sum_recv):
+           near_send, near_recv, sum_send, sum_recv, pass_send, pass_recv):
     width, rows = vectors_ref.shape
     gsz = M // nblk
     cols = width // ncg
@@ -119,11 +119,22 @@
             part[c, m] = total[c * cols : (c + 1) * cols]
     pl.semaphore_wait(barrier, n - 1 + len(others))
 
+    share = rows // nblk
+    lanes = pl.ds(pl.multiple_of(blk * share, share), share)
+
     def codes_copy(k):
-        return remote(codes_ref, codes_all.at[me], send_sem.at[0, k], recv_sem.at[0, k], chip(k))
+        return remote(codes_ref.at[:, lanes], codes_all.at[me, :, lanes], send_sem.at[0, k], recv_sem.at[0, k], chip(k))
 
     def mass_copy(k):
-        return remote(mass_ref, mass_all.at[me], send_sem.at[1, k], recv_sem.at[1, k], chip(k))
+        return remote(mass_ref.at[:, lanes], mass_all.at[me, :, lanes], send_sem.at[1, k], recv_sem.at[1, k], chip(k))
+
+    def across(k):
+        source = lax.rem(me - k + n, n)
+        return [
+            remote(ref.at[source, :, lanes], ref.at[source, :, lanes], pass_send.at[i, k, db], pass_recv.at[i, k, db], team(0, db))
+            for i, ref in enumerate((codes_all, mass_all))
+            for db in range(1, nblk)
+        ]
 
     def piece_copy(k):
         to = lax.rem(me + k, n)
@@ -151,15 +162,27 @@
             hot = spread(codes_all[source, pl.ds(other, 1), :], jnp.ones((1, 1), BF16))
             gram[block(other), :] += lax.dot_general(hot, weighted, NT, preferred_element_type=F32)
 
-    accumulate(me)
-
     def arrive(k):
         codes_copy(k).wait_recv()
         mass_copy(k).wait_recv()
+        for copy in across(k):
+            copy.start()
         piece_copy(k).start()
+
+    def settle(k):
+        for copy in across(k):
+            copy.wait()
         accumulate(lax.rem(me - k + n, n))
 
-    loop(arrive)
+    def turn(k, carry):
+        arrive(k)
+        settle(k - 1)
+        return carry
+
+    accumulate(me)
+    arrive(1)
+    lax.fori_loop(2, n, turn, 0)
+    settle(n - 1)
 
     square = (K, K)
     own = jnp.sum(gram[block(lax.rem(book + 1, M)), :], axis=0, keepdims=True)
@@ -183,22 +206,38 @@
     cut = (cols // 8 + 1) // 2 * 8
     streams = [(i, pl.ds(first, last - first), last - first) for i, (first, last) in enumerate([(0, cut), (cut, cols)]) if last > first]
 
-    def copies(stream, slot):
+    def straight(stream, slot):
         i, span, _ = stream
         here = swap.at[slot, book, span]
-        return [
-            remote(here, here, swap_send.at[slot, i, j], swap_recv.at[slot, i, j], team(dm, db))
+        return {
+            (dm, db): remote(here, here, swap_send.at[slot, i, j], swap_recv.at[slot, i, j], team(dm, db))
             for j, (dm, db) in enumerate(peers)
-        ]
+            if dm == 0 or db == 0
+        }
 
     def send(stream, slot, value):
         swap[slot, book, stream[1]] = value
-        for copy in copies(stream, slot):
+        for copy in straight(stream, slot).values():
             copy.start()
 
     def receive(stream, slot):
-        for copy in copies(stream, slot):
-            copy.wait()
+        i, span, _ = stream
+        direct = straight(stream, slot)
+        relays = []
+        for dm in range(1, gsz):
+            direct[dm, 0].wait_recv()
+            there = swap.at[slot, nblk * flip(member, dm, gsz) + blk, span]
+            for db in range(1, nblk):
+                j = peers.index((dm, db))
+                relay = remote(there, there, swap_send.at[slot, i, j], swap_recv.at[slot, i, j], team(0, db))
+                relay.start()
+                relays.append(relay)
+        for db in range(1, nblk):
+            direct[0, db].wait()
+        for dm in range(1, gsz):
+            direct[dm, 0].wait_send()
+        for relay in relays:
+            relay.wait()
 
     def apply(stream):
         _, span, size = stream
@@ -358,6 +397,8 @@
             dma((ncg, nblk)),
             dma((n,)),
             dma((n,)),
+            dma((2, n, nblk)),
+            dma((2, n, nblk)),
         ],
         compiler_params=pltpu.CompilerParams(collective_id=0, has_side_effects=True),
         name="update",

time: 103 us -> 107 us (1.039)
  Pallas kernels: 96.1 us -> 100 us
    pallas_call x1, Pallas kernels: 96.1 us -> 100 us  [body(): pl.pallas_call(functools.partial(kernel, n, nblk, ncg), out_shape=(shape(...]
where the time goes in v4:
time: 107 us
  Pallas kernels  100 us (93%)
  local copies, waits for them, and re-layouts  4.73 us (4%)
  between operations  1.3 us (1%)
    pallas_call x1, Pallas kernels, body(): pl.pallas_call(functools.partial(kernel, n, nblk, ncg), out_shape=(shape(...  100 us
    unnamed x6, local copies, waits for them, and re-layouts  3.54 us

profile of v4, /device:TPU:0, one launch (start us, length us, event | category | flops | bytes accessed | tf_op | source)
XLA Modules:
  0.0 106.6 jit_solution(2437166707588906466)
XLA Ops:
  1.3 0.0 copy-start.1
  1.3 0.7 copy-done.1
  2.0 0.6 broadcast_in_dim.7
  2.6 100.0 %update.1 = (f32[8,96,256]{2,1,0:T(8,128)}, f32[96,1024]{1,0:T(8,128)}, f32[8,128]{1,0:T(8,128)}) custom-call(f32[1]{0:T(128)S(6)} %copy.9.ridge_ref, s32[8,1024]{1,0:T(8,128)} %bitcast.9, f32[1,1024]{1,0:T(1,128)} %bitcast.10, f32[96,1024]{1,0:T(8,128)} %bitcast.8), custom_call_target="tpu_custom_call" | custom-call | tf_op jit(solution)/shard_map/update/pallas_call | solution.py:370
  102.5 1.2 %slice.3 = f32[1,1]{1,0:T(1,128)} slice(f32[8,128]{1,0:T(8,128)} %get-tuple-element.8), slice={[0:1], [0:1]} | slice | bytes 8 | tf_op jit(solution)/shard_map/slice | solution.py:406
  103.7 0.0 copy-start
  103.7 2.1 %copy.10 = f32[8,256,96]{1,2,0:T(8,128)} copy(f32[8,256,96]{1,2,0:T(8,128)} %bitcast.6) | data formatting | bytes 1572864
  105.8 0.0 copy-done
  105.8 0.7 copy.11
Async XLA Ops:
  1.3 0.7 copy-start.1
  103.7 2.1 %copy-start = (f32[96,1024]{1,0:T(8,128)S(1)}, f32[96,1024]{1,0:T(8,128)}, u32[]{:S(2)}) copy-start(f32[96,1024]{1,0:T(8,128)} %get-tuple-element.7) | copy-start | bytes 1179652
